TPU v7x, 512 devices: a whole 4x4x16 slice. The times are simulated.
512 devices in a mesh: occ: 16 (over y, z_hi), vir: 32 (over x, z_lo, core).
Axes of the slice: x: 4, y: 4, z: 16 (z_hi: 4, z_lo: 4; z = z_hi * 4 + z_lo), core: 2. Of those that a mesh axis runs over, the one named last changes fastest.
Arguments:
- amplitudes: float32 [4, 1024, 1024], P(None, 'occ', 'vir'), may hold values from -6 to 6
- integrals: float32 [4, 28672, 1024], P(None, 'vir', 'occ'), may hold values from -0.1875 to 0.1875
Outputs:
- ladder: float32 [4, 1024, 28672], P(None, 'occ', 'vir')
All inputs are finite; a program needn't handle non-finite values.
Results may differ from a plain program's by a relative error of at most 0.000073.
Values sent between devices are 32-bit elements; how exact they have to be, the bound alone decides.
A program may use at most 64 MiB of HBM per device.

v0:
```python
import jax
import jax.numpy as jnp
from jax import lax
from jax.sharding import PartitionSpec as P


def contract_block(left, piece):
    return lax.dot_general(
        left,
        piece,
        (((2,), (2,)), ((0,), (0,))),
        precision=lax.Precision.HIGHEST,
        preferred_element_type=jnp.float32,
    )


def body(amplitudes, integrals):
    gathered = lax.all_gather(amplitudes, "vir", axis=2, tiled=True)
    panel_sum = contract_block(gathered, lax.all_gather(integrals, "occ", axis=2, tiled=True))
    return 0.5 * panel_sum


def solution(mesh):
    in_specs = (P(None, "occ", "vir"), P(None, "vir", "occ"))
    out_specs = P(None, "occ", "vir")
    return jax.shard_map(body, mesh=mesh, in_specs=in_specs, out_specs=out_specs, check_vma=False)
```

profile of v0, /device:TPU:9, one launch (start us, length us, event | category | flops | bytes accessed | tf_op | source)
XLA Modules:
  0.0 446.1 jit_solution(8332519620568645044)
XLA Ops:
  6.5 0.0 all-gather.3.cloned.1.call-start
  6.5 0.7 all-gather.3.cloned.1.call-update
  7.3 0.0 all-gather.5.cloned.1.call-start
  7.3 0.7 all-gather.5.cloned.1.call-update
  8.0 71.1 %all-gather.3.cloned.1.call-done = f32[4,64,1024]{1,2,0:T(8,128)} async-done(((f32[4,64,32]{1,2,0:T(8,128)}), f32[4,64,1024]{1,2,0:T(8,128)}) %all-gather.3.cloned.1.call-update) | async-done | bytes 1048592 | tf_op jit(solution)/shard_map/all_gather | solution.py:18
  79.1 347.4 %all-gather.5.cloned.1.call-done = f32[4,896,1024]{1,2,0:T(8,128)} async-done(((f32[4,896,64]{1,2,0:T(8,128)}), f32[4,896,1024]{1,2,0:T(8,128)}) %all-gather.5.cloned.1.call-update) | async-done | bytes 14680080 | tf_op jit(solution)/shard_map/all_gather | solution.py:19
  426.6 12.7 %convolution_multiply_fusion = f32[4,64,896]{2,1,0:T(8,128)} fusion(f32[4,64,1024]{1,2,0:T(8,128)} %all-gather.3.cloned.1.call-done, f32[4,896,1024]{1,2,0:T(8,128)} %all-gather.5.cloned.1.call-done), kind=kOutput, calls=%fused_computation | convolution fusion | flops 2818801664 | bytes 16646144 | tf_op jit(solution)/shard_map/dot_general | solution.py:8
Async XLA Ops:
  6.5 72.6 %all-gather.3.cloned.1.call-start = ((), (), s32[]{:S(2)}) async-start(), calls=%async_computation | async-start | bytes 2162688 | tf_op jit(solution)/shard_map/all_gather | solution.py:18
  7.3 419.3 %all-gather.5.cloned.1.call-start = ((), (), s32[]{:S(2)}) async-start(), calls=%async_computation.1 | async-start | bytes 15597568 | tf_op jit(solution)/shard_map/all_gather | solution.py:19
Sparse Core Ops, SparseCore 0:
  9.5 69.5 all-gather.2
  82.1 344.3 all-gather.4
where the time goes:
time: 446 us
  waiting for transfers between devices  420 us (94%)
  between operations  13.4 us (3%)
  matrix products  12.7 us (3%)
    all_gather x1, waiting for transfers between devices, body(): lax.all_gather(integrals, 'occ', axis=2, tiled=True)  347 us
    all_gather x1, waiting for transfers between devices, body(): gathered = lax.all_gather(amplitudes, 'vir', axis=2, tiled=True)  71.1 us
    dot_general x1, matrix products, contract_block(): lax.dot_general(left, piece, (((2,), (2,)), ((0,), (0,))), precision=lax....  12.7 us
  transfers between devices with their start and end apart: 2, of which 2 were waited for; matrix products, arithmetic and copies ran while one was open for 0% of the time, Pallas kernels for 0%

commit v1 on v0

v1 whole, which is shorter than its diff:
```python
import jax
import jax.numpy as jnp
from jax import lax
from jax.experimental import pallas as pl
from jax.experimental.pallas import tpu as pltpu
from jax.sharding import PartitionSpec as P

MESH = pl.DeviceIdType.MESH
CHUNK = 128
AHEAD = 3
LAG = 4


def kernel(
    at_ref, bt_ref, out_ref, pk, ag, at, a_hi, a_lo, bt, cb,
    a_send, a_recv, b_send, b_recv, up_send, up_recv, dn_send, dn_recv, ru_send, rd_send, far_recv, c_send, c_recv,
):
    o, v = lax.axis_index("occ"), lax.axis_index("vir")
    y, zh = o // 4, o % 4
    x, zl, c = v // 8, (v // 2) % 4, v % 2
    z = zh * 4 + zl
    zc = (z + 14) % 16
    g, zs = zc // 4, zc % 4
    chunks = bt.shape[0]
    y_up, y_dn = (y + 1) % 4, (y + 3) % 4

    def device(z_, y_=y, x_=x, c_=c):
        w = z_ % 16
        return (y_ * 4 + w // 4, (x_ * 4 + w % 4) * 2 + c_)

    def remote(src, dst, send, recv, where):
        return pltpu.make_async_remote_copy(
            src_ref=src, dst_ref=dst, send_sem=send, recv_sem=recv, device_id=where, device_id_type=MESH
        )

    def drain(ref, sem):
        pltpu.make_async_copy(ref, ref, sem).wait()

    pk[:, :, 0:64] = at_ref[:, 0:16, :]
    pk[:, :, 64:128] = at_ref[:, 16:32, :]

    barrier = pltpu.get_barrier_semaphore()
    greet = [device(z + d) for d in (2, 6, 10, 14)]
    greet += [device(4 * g + 2 + (zs + d) % 4) for d in (1, 2, 3)]
    greet += [device(z, y_=y_up), device(z, y_=y_dn)]
    greet += [device(z, x_=(x + d) % 4) for d in (1, 2, 3)]
    greet += [device(z, c_=1 - c)]
    for where in greet:
        pl.semaphore_signal(barrier, inc=1, device_id=where, device_id_type=MESH)
    pl.semaphore_wait(barrier, len(greet))

    def lanes(s):
        return pl.ds(pl.multiple_of(s * CHUNK, CHUNK), CHUNK)

    def rows(start, size):
        return pl.ds(pl.multiple_of(start, 64), size)

    def send_b(s):
        for h in range(4):
            remote(
                bt_ref.at[h, :, lanes(s)], bt.at[s, rows(o * 64, 64)], b_send, b_recv.at[s], device(zl + 4 * h + 2)
            ).start()

    for h in range(4):
        remote(pk.at[h], ag.at[c, x, zl, zh], a_send.at[0], a_recv.at[0], device(zl + 4 * h + 2)).start()
    for s in range(AHEAD):
        send_b(s)

    own = rows(y * 256, 256)
    from_dn = rows(y_dn * 256, 256)
    from_up = rows(y_up * 256, 256)
    far = rows(((y + 2) % 4) * 256, 256)
    up_half = rows(y_dn * 256, 128)
    dn_half = rows(y_up * 256 + 128, 128)

    def step(s, carry):
        @pl.when(s < chunks)
        def _():
            drain(bt.at[s, own], b_recv.at[s])
            remote(bt.at[s, own], bt.at[s, own], up_send, up_recv.at[s], device(z, y_=y_up)).start()
            remote(bt.at[s, own], bt.at[s, own], dn_send, dn_recv.at[s], device(z, y_=y_dn)).start()

        @pl.when(s == 0)
        def _():
            drain(ag.at[c, x, zs], a_recv.at[0])
            for d in (1, 2, 3):
                there = device(4 * g + 2 + (zs + d) % 4)
                remote(ag.at[c, x, zs], ag.at[c, x, zs], a_send.at[1], a_recv.at[1], there).start()

        @pl.when(s + AHEAD < chunks)
        def _():
            send_b(s + AHEAD)

        @pl.when(jnp.logical_and(s >= 1, s < chunks + 1))
        def _():
            t = s - 1
            drain(bt.at[t, from_dn], up_recv.at[t])
            remote(bt.at[t, up_half], bt.at[t, up_half], ru_send, far_recv.at[t], device(z, y_=y_up)).start()
            drain(bt.at[t, from_up], dn_recv.at[t])
            remote(bt.at[t, dn_half], bt.at[t, dn_half], rd_send, far_recv.at[t], device(z, y_=y_dn)).start()

        @pl.when(s == 2)
        def _():
            drain(ag.at[c, x, pl.ds(0, 3)], a_recv.at[1])
            for d in (1, 2, 3):
                there = device(z, x_=(x + d) % 4)
                remote(ag.at[c, x], ag.at[c, x], a_send.at[2], a_recv.at[2], there).start()

        @pl.when(s == 3)
        def _():
            drain(ag.at[c, pl.ds(0, 3)], a_recv.at[2])
            remote(ag.at[c], ag.at[c], a_send.at[3], a_recv.at[3], device(z, c_=1 - c)).start()

        @pl.when(s == LAG)
        def _():
            drain(ag.at[1 - c], a_recv.at[3])

            def unpack(u, carry):
                low = lax.broadcasted_iota(jnp.int32, (16, 128), 1) < 64
                part = [ag[u % 2, u // 8, (u // 2) % 4, h] for h in range(4)]
                turned = [pltpu.roll(p, 64, 1) for p in part]
                for h in (0, 2):
                    side = pl.ds(64 * h, 128)
                    at[pl.ds(pl.multiple_of(u * 32, 16), 16), side] = jnp.where(low, part[h], turned[h + 1])
                    at[pl.ds(pl.multiple_of(u * 32 + 16, 16), 16), side] = jnp.where(low, turned[h], part[h + 1])
                return carry

            lax.fori_loop(0, 32, unpack, 0)

            def turn(k, carry):
                block = at[pl.ds(pl.multiple_of(k * 128, 128), 128), :].T
                high = block.astype(jnp.bfloat16)
                a_hi[:, pl.ds(pl.multiple_of(k * 128, 128), 128)] = high
                a_lo[:, pl.ds(pl.multiple_of(k * 128, 128), 128)] = (block - high.astype(jnp.float32)).astype(jnp.bfloat16)
                return carry

            lax.fori_loop(0, 8, turn, 0)

        @pl.when(s >= LAG)
        def _():
            t = s - LAG
            drain(bt.at[t, far], far_recv.at[t])
            block = bt[t]
            high = block.astype(jnp.bfloat16)
            low = (block - high.astype(jnp.float32)).astype(jnp.bfloat16)
            both = jnp.dot(a_hi[...], jnp.concatenate([high, low], axis=1), preferred_element_type=jnp.float32)
            cross = jnp.dot(a_lo[...], high, preferred_element_type=jnp.float32)
            cb[t] = 0.5 * (both[:, 0:CHUNK] + (both[:, CHUNK:] + cross))
            for h in range(4):
                remote(
                    cb.at[t, pl.ds(64 * h, 64)], out_ref.at[g, :, lanes(t)], c_send, c_recv, device(4 * h + zs)
                ).start()

        return carry

    lax.fori_loop(0, chunks + LAG, step, 0)

    drain(out_ref, c_recv)
    drain(pk, a_send.at[0])
    drain(ag.at[c, x, pl.ds(0, 3)], a_send.at[1])
    drain(ag.at[c, pl.ds(0, 3)], a_send.at[2])
    drain(ag.at[c], a_send.at[3])
    drain(bt_ref, b_send)
    drain(cb, up_send)
    drain(cb, dn_send)
    drain(cb.at[:, pl.ds(0, 128)], ru_send)
    drain(cb.at[:, pl.ds(0, 128)], rd_send)
    drain(cb, c_send)


def body(amplitudes, integrals):
    at = jnp.swapaxes(amplitudes, 1, 2)
    bt = jnp.swapaxes(integrals, 1, 2)
    n_g, depth, cols = bt.shape
    chunks = cols // CHUNK
    f32, bf16 = jnp.float32, jnp.bfloat16
    dma = pltpu.SemaphoreType.DMA
    return pl.pallas_call(
        kernel,
        out_shape=jax.ShapeDtypeStruct((n_g, 64, cols), f32),
        in_specs=[pl.BlockSpec(memory_space=pltpu.VMEM), pl.BlockSpec(memory_space=pl.ANY)],
        out_specs=pl.BlockSpec(memory_space=pl.ANY),
        scratch_shapes=[
            pltpu.VMEM((4, 16, 128), f32),
            pltpu.VMEM((2, 4, 4, 4, 16, 128), f32),
            pltpu.VMEM((1024, 256), f32),
            pltpu.VMEM((256, 1024), bf16),
            pltpu.VMEM((256, 1024), bf16),
            pltpu.VMEM((chunks, 1024, CHUNK), f32),
            pltpu.VMEM((chunks, 256, CHUNK), f32),
            dma((4,)),
            dma((4,)),
            dma,
            dma((chunks,)),
            dma,
            dma((chunks,)),
            dma,
            dma((chunks,)),
            dma,
            dma,
            dma((chunks,)),
            dma,
            dma,
        ],
        compiler_params=pltpu.CompilerParams(collective_id=0, has_side_effects=True),
    )(at, bt)


def solution(mesh):
    in_specs = (P(None, "occ", "vir"), P(None, "vir", "occ"))
    out_specs = P(None, "occ", "vir")
    return jax.shard_map(body, mesh=mesh, in_specs=in_specs, out_specs=out_specs, check_vma=False)
```

time: 446 us -> 104 us (0.23)
  the two profiles are of different devices: /device:TPU:9 before, /device:TPU:88 now
where the time goes in v1:
time: 104 us; the launch traced here: 103 us
  Pallas kernels  101 us (97%)
  local copies, waits for them, and re-layouts  2.16 us (2%)
    pallas_call x1, Pallas kernels, body(): pl.pallas_call(kernel, out_shape=jax.ShapeDtypeStruct((n_g, 64, cols), f3...  101 us
    unnamed x1, local copies, waits for them, and re-layouts  2.16 us

profile of v1, /device:TPU:88, one launch (start us, length us, event | category | flops | bytes accessed | tf_op | source)
XLA Modules:
  0.0 102.8 jit_solution(16471443151493601386)
XLA Ops:
  0.0 100.7 %shard_map.28 = f32[4,64,896]{2,1,0:T(8,128)} custom-call(f32[4,32,64]{2,1,0:T(8,128)} %bitcast.3, f32[4,64,896]{2,1,0:T(8,128)} %bitcast.2), custom_call_target="tpu_custom_call" | custom-call | tf_op jit(solution)/shard_map/pallas_call | solution.py:178
  100.7 2.2 %copy.4 = f32[4,64,896]{2,1,0:T(8,128)} copy(f32[4,64,896]{2,1,0:T(8,128)} %shard_map.28) | data formatting | bytes 1835008

commit v2 on v1

--- a/solution.py
+++ b/solution.py
@@ -9,6 +9,7 @@
 CHUNK = 128
 AHEAD = 3
 LAG = 4
+ORDER = (1, 2, 0, 3)
 
 
 def kernel(
@@ -56,12 +57,14 @@
         return pl.ds(pl.multiple_of(start, 64), size)
 
     def send_b(s):
-        for h in range(4):
+        for i in ORDER:
+            h = (zh + i) % 4
             remote(
                 bt_ref.at[h, :, lanes(s)], bt.at[s, rows(o * 64, 64)], b_send, b_recv.at[s], device(zl + 4 * h + 2)
             ).start()
 
-    for h in range(4):
+    for i in ORDER:
+        h = (zh + i) % 4
         remote(pk.at[h], ag.at[c, x, zl, zh], a_send.at[0], a_recv.at[0], device(zl + 4 * h + 2)).start()
     for s in range(AHEAD):
         send_b(s)
@@ -146,9 +149,10 @@
             both = jnp.dot(a_hi[...], jnp.concatenate([high, low], axis=1), preferred_element_type=jnp.float32)
             cross = jnp.dot(a_lo[...], high, preferred_element_type=jnp.float32)
             cb[t] = 0.5 * (both[:, 0:CHUNK] + (both[:, CHUNK:] + cross))
-            for h in range(4):
+            for i in ORDER:
+                h = ((z + 2 + 4 * i) % 16) // 4
                 remote(
-                    cb.at[t, pl.ds(64 * h, 64)], out_ref.at[g, :, lanes(t)], c_send, c_recv, device(4 * h + zs)
+                    cb.at[t, rows(64 * h, 64)], out_ref.at[g, :, lanes(t)], c_send, c_recv, device(4 * h + zs)
                 ).start()
 
         return carry
@@ -170,7 +174,7 @@
 
 def body(amplitudes, integrals):
     at = jnp.swapaxes(amplitudes, 1, 2)
-    bt = jnp.swapaxes(integrals, 1, 2)
+    bt = pltpu.with_memory_space_constraint(jnp.swapaxes(integrals, 1, 2), pltpu.HBM)
     n_g, depth, cols = bt.shape
     chunks = cols // CHUNK
     f32, bf16 = jnp.float32, jnp.bfloat16
@@ -202,7 +206,7 @@
             dma,
             dma,
         ],
-        compiler_params=pltpu.CompilerParams(collective_id=0, has_side_effects=True),
+        compiler_params=pltpu.CompilerParams(collective_id=0, has_side_effects=True, vmem_limit_bytes=20 * 2**20),
     )(at, bt)
 
 

time: 104 us -> 101 us (0.971)
  the two profiles are of different devices: /device:TPU:88 before, /device:TPU:80 now
where the time goes in v2:
time: 101 us
  Pallas kernels  99.6 us (99%)
  local copies, waits for them, and re-layouts  1.76 us (2%)
    pallas_call x1, Pallas kernels, body(): pl.pallas_call(kernel, out_shape=jax.ShapeDtypeStruct((n_g, 64, cols), f3...  99.6 us

profile of v2, /device:TPU:80, one launch (start us, length us, event | category | flops | bytes accessed | tf_op | source)
XLA Modules:
  0.0 101.3 jit_solution(2321564485459131965)
XLA Ops:
  0.0 0.0 copy-start
  0.0 0.8 copy-done
  0.8 99.6 %shard_map.28 = f32[4,64,896]{2,1,0:T(8,128)S(1)} custom-call(f32[4,32,64]{2,1,0:T(8,128)S(1)} %bitcast.2, f32[4,64,896]{2,1,0:T(8,128)} %bitcast.3), custom_call_target="tpu_custom_call" | custom-call | tf_op jit(solution)/shard_map/pallas_call | solution.py:182
  100.4 0.9 copy.4
Async XLA Ops:
  0.0 0.8 copy-start

commit v3 on v2

--- a/solution.py
+++ b/solution.py
@@ -13,8 +13,8 @@
 
 
 def kernel(
-    at_ref, bt_ref, out_ref, pk, ag, at, a_hi, a_lo, bt, cb,
-    a_send, a_recv, b_send, b_recv, up_send, up_recv, dn_send, dn_recv, ru_send, rd_send, far_recv, c_send, c_recv,
+    at_ref, bt_ref, out_ref, an, pk, ag, at, a_hi, a_lo, bt, cb,
+    a_send, a_recv, b_send, b_recv, up_send, up_recv, dn_send, dn_recv, ru_send, rd_send, far_recv, c_send, c_recv, fetched,
 ):
     o, v = lax.axis_index("occ"), lax.axis_index("vir")
     y, zh = o // 4, o % 4
@@ -37,17 +37,19 @@
     def drain(ref, sem):
         pltpu.make_async_copy(ref, ref, sem).wait()
 
-    pk[:, :, 0:64] = at_ref[:, 0:16, :]
-    pk[:, :, 64:128] = at_ref[:, 16:32, :]
-
     barrier = pltpu.get_barrier_semaphore()
-    greet = [device(z + d) for d in (2, 6, 10, 14)]
+    greet = [device(z + d) for d in (6, 10, 2, 14)]
     greet += [device(4 * g + 2 + (zs + d) % 4) for d in (1, 2, 3)]
     greet += [device(z, y_=y_up), device(z, y_=y_dn)]
     greet += [device(z, x_=(x + d) % 4) for d in (1, 2, 3)]
     greet += [device(z, c_=1 - c)]
     for where in greet:
         pl.semaphore_signal(barrier, inc=1, device_id=where, device_id_type=MESH)
+    fetch = pltpu.make_async_copy(at_ref, an, fetched)
+    fetch.start()
+    fetch.wait()
+    pk[:, :, 0:64] = an[:, 0:16, :]
+    pk[:, :, 64:128] = an[:, 16:32, :]
     pl.semaphore_wait(barrier, len(greet))
 
     def lanes(s):
@@ -173,7 +175,7 @@
 
 
 def body(amplitudes, integrals):
-    at = jnp.swapaxes(amplitudes, 1, 2)
+    at = pltpu.with_memory_space_constraint(jnp.swapaxes(amplitudes, 1, 2), pltpu.HBM)
     bt = pltpu.with_memory_space_constraint(jnp.swapaxes(integrals, 1, 2), pltpu.HBM)
     n_g, depth, cols = bt.shape
     chunks = cols // CHUNK
@@ -182,9 +184,10 @@
     return pl.pallas_call(
         kernel,
         out_shape=jax.ShapeDtypeStruct((n_g, 64, cols), f32),
-        in_specs=[pl.BlockSpec(memory_space=pltpu.VMEM), pl.BlockSpec(memory_space=pl.ANY)],
+        in_specs=[pl.BlockSpec(memory_space=pl.ANY), pl.BlockSpec(memory_space=pl.ANY)],
         out_specs=pl.BlockSpec(memory_space=pl.ANY),
         scratch_shapes=[
+            pltpu.VMEM((4, 32, 64), f32),
             pltpu.VMEM((4, 16, 128), f32),
             pltpu.VMEM((2, 4, 4, 4, 16, 128), f32),
             pltpu.VMEM((1024, 256), f32),
@@ -205,6 +208,7 @@
             dma((chunks,)),
             dma,
             dma,
+            dma,
         ],
         compiler_params=pltpu.CompilerParams(collective_id=0, has_side_effects=True, vmem_limit_bytes=20 * 2**20),
     )(at, bt)

time: 101 us -> 101 us (level)
  the two profiles are of different devices: /device:TPU:80 before, /device:TPU:88 now
where the time goes in v3:
time: 101 us
  Pallas kernels  99.6 us (99%)
    pallas_call x1, Pallas kernels, body(): pl.pallas_call(kernel, out_shape=jax.ShapeDtypeStruct((n_g, 64, cols), f3...  99.6 us

profile of v3, /device:TPU:88, one launch (start us, length us, event | category | flops | bytes accessed | tf_op | source)
XLA Modules:
  0.0 100.5 jit_solution(11898718833145566316)
XLA Ops:
  0.0 99.6 %shard_map.28 = f32[4,64,896]{2,1,0:T(8,128)S(1)} custom-call(f32[4,32,64]{2,1,0:T(8,128)} %bitcast.3, f32[4,64,896]{2,1,0:T(8,128)} %bitcast.2), custom_call_target="tpu_custom_call" | custom-call | tf_op jit(solution)/shard_map/pallas_call | solution.py:184
  99.6 0.9 copy.4
